TPU v7x, 256 devices: a whole 4x4x8 slice. The times are simulated.
256 devices in a mesh: buoy: 4 (over x), dom: 64 (over z, y, core).
Axes of the slice: x: 4, y: 4, z: 8, core: 2. Of those that a mesh axis runs over, the one named last changes fastest.
Arguments:
- ambient: float32 [32, 36, 448], P('buoy', None, 'dom'), may hold values from -6 to 6
- initial_out: float32 [32, 36, 448], P('buoy', None, 'dom'), may hold values from -6 to 6
- translation: bfloat16 [512, 448, 448], P(('buoy', 'dom')), may hold values from -0.0625 to 0.0625
- pair_source: int32 [512], P(('buoy', 'dom')), may hold values from 0 to 31, as said below
- pair_target: int32 [512], P(('buoy', 'dom')), may hold values from 0 to 31, as said below
- pair_live: int32 [512], P(('buoy', 'dom')), may hold values from 0 to 1, as said below
- diffract: bfloat16 [448, 448], P('dom'), may hold values from -0.25 to 0.25
- panel_rows: bfloat16 [8192, 448], P('dom'), may hold values from -0.25 to 0.25
Outputs:
- outgoing: float32 [32, 36, 448], P('buoy', None, 'dom')
- sources: bfloat16 [32, 36, 8192], P('buoy', None, 'dom')
Inputs may be any that keep to these rules, and one draw needn't show every extreme that they name: `pair_target`: the slots of one device name target buoys among the 8 buoys of its index of buoy. `pair_source`: A source buoy differs from its target by 1 to 8 places in the farm's order; the live slots of one target name distinct sources. `pair_live`: A slot is live exactly where its source lies inside the farm; some device has all 2 live.
All inputs are finite; a program needn't handle non-finite values.
Results may differ from a plain program's by a relative error of at most 0.015.
Values may be sent and summed in bfloat16 or wider, within the bound.
No kernel may reach another device: no remote copies, remote signals or barrier semaphores. Data moves between devices by JAX's collectives and lax.ppermute only.
A program may use at most 64 MiB of HBM per device.

v0:
```python
import jax
import jax.numpy as jnp
from jax import lax
from jax.sharding import PartitionSpec as P

ITERS = 2


def extended_2(block, sides, width):
    for axis, dim in sides:
        count = lax.axis_size(axis)
        forward = [(i, i + 1) for i in range(count - 1)]
        backward = [(target, source) for source, target in forward]
        low = lax.ppermute(
            lax.slice_in_dim(block, block.shape[dim] - width, None, axis=dim), axis, forward
        )
        high = lax.ppermute(lax.slice_in_dim(block, 0, width, axis=dim), axis, backward)
        block = jnp.concatenate([low, block, high], axis=dim)
    return block


def rows_product(left, right):
    return lax.dot_general(
        left, right, (((1,), (1,)), ((), ())), preferred_element_type=jnp.float32
    )


def shards(
    ambient, initial_out, translation, pair_source, pair_target, pair_live, diffract, panel_rows
):
    per_dev, headings, share_width = initial_out.shape
    full_width = translation.shape[1]
    first_buoy = lax.axis_index("buoy") * per_dev
    column_start = lax.axis_index("dom") * share_width
    rows_source = pair_source - (first_buoy - per_dev)
    rows_target = pair_target - first_buoy
    place_table = (
        (rows_target[None, :] == jnp.arange(per_dev, dtype=jnp.int32)[:, None])
        & (pair_live[None, :] == 1)
    ).astype(jnp.float32)
    matrices = translation.astype(jnp.float32)
    coeffs = initial_out
    incident_bf = None
    for step in range(ITERS):
        whole = lax.all_gather(coeffs, "dom", axis=2, tiled=True)
        extended = extended_2(whole.astype(jnp.bfloat16), (("buoy", 0),), per_dev).astype(
            whole.dtype
        )
        picked = jnp.take(extended, rows_source, axis=0)
        terms = jnp.einsum("phn,pmn->phm", picked, matrices, precision=lax.Precision.HIGHEST)
        partial_value = jnp.einsum(
            "kp,phm->khm", place_table, terms, precision=lax.Precision.HIGHEST
        )
        own_columns = (
            lax.dynamic_slice_in_dim(partial_value, column_start, share_width, 2) + ambient
        )
        partial_value = lax.dynamic_update_slice_in_dim(partial_value, own_columns, column_start, 2)
        incident = lax.psum(partial_value, "dom")
        incident_bf = incident.astype(jnp.bfloat16)
        flat = incident_bf.reshape(per_dev * headings, full_width)
        coeffs = rows_product(flat, diffract).reshape(per_dev, headings, share_width)
    flat = incident_bf.reshape(per_dev * headings, full_width)
    sources = (
        rows_product(flat, panel_rows)
        .astype(jnp.bfloat16)
        .reshape(per_dev, headings, panel_rows.shape[0])
    )
    return (coeffs, sources)


def solution(mesh):
    in_specs = (
        P("buoy", None, "dom"),
        P("buoy", None, "dom"),
        P(("buoy", "dom"), None, None),
        P(("buoy", "dom")),
        P(("buoy", "dom")),
        P(("buoy", "dom")),
        P("dom", None),
        P("dom", None),
    )
    out_specs = (P("buoy", None, "dom"), P("buoy", None, "dom"))
    return jax.shard_map(shards, mesh=mesh, in_specs=in_specs, out_specs=out_specs, check_vma=False)
```

profile of v0, /device:TPU:6, one launch (start us, length us, event | category | flops | bytes accessed | tf_op | source)
XLA Modules:
  0.0 659.2 jit_solution(17983448239093237719)
XLA Ops:
  0.7 0.8 convert.2
  1.5 53.9 %all_gather.6 = bf16[8,36,448]{1,0,2:T(8,128)(2,1)S(1)} all-gather(bf16[8,36,7]{1,0,2:T(8,128)(2,1)S(1)} %convert.2), channel_id=1, replica_groups=mesh['buoy'=4,'dom'=64] {'dom'}, dimensions={2}, use_global_device_ids=true | all-gather | bytes 262080 | tf_op jit(solution)/shard_map/all_gather | solution.py:45
  55.4 0.7 copy.70
  56.1 2.7 collective-permute-start.1
  58.9 1.3 collective-permute-start
  60.4 5.9 collective-permute-done.1
  66.3 0.7 copy-done.1
  67.0 3.5 collective-permute-done
  70.6 1.3 maximum_convert_fusion
  72.4 0.9 fusion.4
  74.0 0.6 dynamic_update_slice.6
  74.6 258.2 %all-reduce.2 = bf16[8,36,448]{2,0,1:T(8,128)(2,1)S(1)} all-reduce(f32[8,36,448]{2,0,1:T(8,128)S(1)} %dynamic_update_slice.6), channel_id=1, replica_groups=mesh['buoy'=4,'dom'=64] {'dom'}, use_global_device_ids=true, to_apply=%region_0.0 | all-reduce | flops 129024 | bytes 774144 | tf_op jit(solution)/shard_map/psum | solution.py:58
  333.2 47.3 %all_gather.7 = bf16[8,36,448]{1,0,2:T(8,128)(2,1)S(1)} all-gather(bf16[8,36,7]{1,0,2:T(8,128)(2,1)S(1)} %copy.74), channel_id=1, replica_groups=mesh['buoy'=4,'dom'=64] {'dom'}, dimensions={2}, use_global_device_ids=true | all-gather | bytes 262080 | tf_op jit(solution)/shard_map/all_gather | solution.py:45
  380.5 0.9 copy.75
  381.4 2.4 collective-permute-start.3
  383.9 1.5 collective-permute-start.2
  385.3 5.3 collective-permute-done.3
  390.6 4.1 collective-permute-done.2
  395.0 1.0 copy.76
  396.6 0.9 fusion.2
  398.2 0.6 dynamic_update_slice.7
  398.8 258.3 %all-reduce.3 = bf16[8,36,448]{2,0,1:T(8,128)(2,1)S(1)} all-reduce(f32[8,36,448]{2,0,1:T(8,128)S(1)} %dynamic_update_slice.7), channel_id=1, replica_groups=mesh['buoy'=4,'dom'=64] {'dom'}, use_global_device_ids=true, to_apply=%region_1.3 | all-reduce | flops 129024 | bytes 774144 | tf_op jit(solution)/shard_map/psum | solution.py:58
  657.5 0.6 copy.81
  658.5 0.6 copy.82
  (34 shorter events, 4.0 us)
Async XLA Ops:
  0.6 71.8 %copy-start = (bf16[2,448,448]{2,1,0:T(8,128)(2,1)S(1)}, bf16[2,448,448]{2,1,0:T(8,128)(2,1)}, u32[]{:S(2)}) copy-start(bf16[2,448,448]{2,1,0:T(8,128)(2,1)} %param.12) | copy-start | bytes 2408452
  0.6 59.5 %copy-start.6 = (s32[2]{0:T(128)S(1)}, s32[2]{0:T(128)}, u32[]{:S(2)}) copy-start(s32[2]{0:T(128)} %param.14) | copy-start | bytes 28
  0.7 59.5 %copy-start.4 = (s32[2]{0:T(128)S(1)}, s32[2]{0:T(128)}, u32[]{:S(2)}) copy-start(s32[2]{0:T(128)} %param.13) | copy-start | bytes 28
  0.7 59.6 %copy-start.3 = (f32[8,36,7]{1,0,2:T(8,128)S(1)}, f32[8,36,7]{1,0,2:T(8,128)}, u32[]{:S(2)}) copy-start(f32[8,36,7]{1,0,2:T(8,128)} %param.10) | copy-start | bytes 24196
  0.7 59.7 %copy-start.7 = (s32[2]{0:T(128)S(1)}, s32[2]{0:T(128)}, u32[]{:S(2)}) copy-start(s32[2]{0:T(128)} %param.15) | copy-start | bytes 28
  56.1 10.2 %collective-permute-start.1 = (bf16[8,36,448]{2,1,0:T(8,128)(2,1)S(1)}, bf16[8,36,448]{2,1,0:T(8,128)(2,1)S(1)}, u32[]{:S(2)}, u32[]{:S(2)}) collective-permute-start(bf16[8,36,448]{2,1,0:T(8,128)(2,1)S(1)} %copy.70), channel_id=1, source_target_pairs={{64,0},{128,64},{192,128},{65,1},{129,65},{193,129},{66,2},{130,66... | collective-permute-start | bytes 774152 | tf_op jit(solution)/shard_map/ppermute | solution.py:17
  58.9 11.7 %collective-permute-start = (bf16[8,36,448]{2,1,0:T(8,128)(2,1)S(1)}, bf16[8,36,448]{2,1,0:T(8,128)(2,1)}, u32[]{:S(2)}, u32[]{:S(2)}) collective-permute-start(bf16[8,36,448]{2,1,0:T(8,128)(2,1)S(1)} %copy.70), channel_id=1, source_target_pairs={{0,64},{64,128},{128,192},{1,65},{65,129},{129,193},{2,66},{66,130... | collective-permute-start | bytes 774152 | tf_op jit(solution)/shard_map/ppermute | solution.py:14
  66.3 0.7 copy-start.1
  72.4 260.5 %copy-start.5 = (bf16[7,448]{1,0:T(8,128)(2,1)S(1)}, bf16[7,448]{1,0:T(8,128)(2,1)}, u32[]{:S(2)}) copy-start(bf16[7,448]{1,0:T(8,128)(2,1)} %param.16) | copy-start | bytes 18820
  381.4 9.2 %collective-permute-start.3 = (bf16[8,36,448]{2,0,1:T(8,128)(2,1)S(1)}, bf16[8,36,448]{2,0,1:T(8,128)(2,1)S(1)}, u32[]{:S(2)}, u32[]{:S(2)}) collective-permute-start(bf16[8,36,448]{2,0,1:T(8,128)(2,1)S(1)} %copy.75), channel_id=1, source_target_pairs={{64,0},{128,64},{192,128},{65,1},{129,65},{193,129},{66,2},{130,66... | collective-permute-start | bytes 774152 | tf_op jit(solution)/shard_map/ppermute | solution.py:17
  383.9 10.9 %collective-permute-start.2 = (bf16[8,36,448]{2,0,1:T(8,128)(2,1)S(1)}, bf16[8,36,448]{2,0,1:T(8,128)(2,1)S(1)}, u32[]{:S(2)}, u32[]{:S(2)}) collective-permute-start(bf16[8,36,448]{2,0,1:T(8,128)(2,1)S(1)} %copy.75), channel_id=1, source_target_pairs={{0,64},{64,128},{128,192},{1,65},{65,129},{129,193},{2,66},{66,130... | collective-permute-start | bytes 774152 | tf_op jit(solution)/shard_map/ppermute | solution.py:14
  398.1 260.2 %copy-start.2 = (bf16[128,448]{0,1:T(8,128)(2,1)S(1)}, bf16[128,448]{0,1:T(8,128)(2,1)}, u32[]{:S(2)}) copy-start(bf16[128,448]{0,1:T(8,128)(2,1)} %param.17) | copy-start | bytes 344068
where the time goes:
time: 659 us
  blocking collectives  618 us (94%)
  waiting for transfers between devices  18.8 us (3%)
  starting transfers between devices  7.95 us (1%)
  local copies, waits for them, and re-layouts  7.34 us (1%)
    psum x2, blocking collectives, shards(): incident = lax.psum(partial_value, 'dom')  517 us
    all_gather x2, blocking collectives, shards(): whole = lax.all_gather(coeffs, 'dom', axis=2, tiled=True)  101 us
  transfers between devices with their start and end apart: 4, of which 4 were waited for; matrix products, arithmetic and copies ran while one was open for 0% of the time, Pallas kernels for 0%

commit v1 on v0

--- a/solution.py
+++ b/solution.py
@@ -55,7 +55,7 @@
             lax.dynamic_slice_in_dim(partial_value, column_start, share_width, 2) + ambient
         )
         partial_value = lax.dynamic_update_slice_in_dim(partial_value, own_columns, column_start, 2)
-        incident = lax.psum(partial_value, "dom")
+        incident = jnp.sum(lax.all_gather(partial_value, "dom"), axis=0)
         incident_bf = incident.astype(jnp.bfloat16)
         flat = incident_bf.reshape(per_dev * headings, full_width)
         coeffs = rows_product(flat, diffract).reshape(per_dev, headings, share_width)

time: 659 us -> 499 us (0.76)
  blocking collectives: 618 us -> 103 us
  waiting for transfers between devices: 18.8 us -> 329 us
  other arithmetic: 2.58 us -> 29.8 us
  between operations: 0.97 us -> 14.4 us
    psum x2 -> x0, blocking collectives: 517 us -> none  [shards(): incident = lax.psum(partial_value, 'dom')]
    all_gather x0 -> x2, waiting for transfers between devices: none -> 311 us  [shards(): incident = jnp.sum(lax.all_gather(partial_value, 'dom'), axis=0)]
    reduce_sum x0 -> x2, other arithmetic: none -> 27.3 us  [shards(): incident = jnp.sum(lax.all_gather(partial_value, 'dom'), axis=0)]
  transfers between devices with their start and end apart: 4 -> 6, of which waited for: 4 -> 6; matrix products, arithmetic and copies ran while one was open for 0% -> 0% of each run, Pallas kernels for 0% -> 0%
where the time goes in v1:
time: 499 us; the launch traced here: 497 us
  waiting for transfers between devices  329 us (66%)
  blocking collectives  103 us (21%)
  other arithmetic  29.8 us (6%)
  between operations  14.4 us (3%)
  local copies, waits for them, and re-layouts  8.95 us (2%)
  starting transfers between devices  8.36 us (2%)
    all_gather x2, waiting for transfers between devices, shards(): incident = jnp.sum(lax.all_gather(partial_value, 'dom'), axis=0)  311 us
    all_gather x2, blocking collectives, shards(): whole = lax.all_gather(coeffs, 'dom', axis=2, tiled=True)  103 us
    reduce_sum x2, other arithmetic, shards(): incident = jnp.sum(lax.all_gather(partial_value, 'dom'), axis=0)  27.3 us
    ppermute x2, waiting for transfers between devices, extended_2(): lax.ppermute(lax.slice_in_dim(block, 0, width, axis=dim), axis, backward)  11.1 us
  transfers between devices with their start and end apart: 6, of which 6 were waited for; matrix products, arithmetic and copies ran while one was open for 0% of the time, Pallas kernels for 0%

profile of v1, /device:TPU:6, one launch (start us, length us, event | category | flops | bytes accessed | tf_op | source)
XLA Modules:
  0.0 497.4 jit_solution(6649758735471909923)
XLA Ops:
  7.3 0.8 convert.2
  8.1 53.9 %all_gather.22 = bf16[8,36,448]{1,0,2:T(8,128)(2,1)S(1)} all-gather(bf16[8,36,7]{1,0,2:T(8,128)(2,1)S(1)} %convert.2), channel_id=1, replica_groups=mesh['buoy'=4,'dom'=64] {'dom'}, dimensions={2}, use_global_device_ids=true | all-gather | bytes 262080 | tf_op jit(solution)/shard_map/all_gather | solution.py:45
  62.0 0.7 copy.65
  62.7 2.7 collective-permute-start.1
  65.4 1.3 collective-permute-start
  67.0 5.9 %collective-permute-done.1 = bf16[8,36,448]{2,1,0:T(8,128)(2,1)S(1)} collective-permute-done((bf16[8,36,448]{2,1,0:T(8,128)(2,1)S(1)}, bf16[8,36,448]{2,1,0:T(8,128)(2,1)S(1)}, u32[]{:S(2)}, u32[]{:S(2)}) %collective-permute-start.1) | collective-permute-done | bytes 258080 | tf_op jit(solution)/shard_map/ppermute | solution.py:17
  72.9 0.7 copy-done.4
  73.6 3.5 collective-permute-done
  77.1 1.3 maximum_convert_fusion
  79.0 0.9 fusion.4
  81.2 0.8 copy-done.3
  82.1 155.0 %all-gather.3.cloned.1.call-done = f32[64,8,36,448]{3,1,2,0:T(8,128)} async-done(((f32[1,8,36,448]{3,1,2,0:T(8,128)}), f32[64,8,36,448]{3,1,2,0:T(8,128)}) %all-gather.3.cloned.1.call-update) | async-done | bytes 33030160 | tf_op jit(solution)/shard_map/all_gather | solution.py:58
  237.1 13.6 %reduce_sum.18 = bf16[8,36,448]{2,0,1:T(8,128)(2,1)S(1)} reduce(f32[64,8,36,448]{3,1,2,0:T(8,128)} %all-gather.3.cloned.1.call-done, f32[]{:T(128)} %constant.34.clone.1), dimensions={0}, to_apply=%region_0.0 | reduce | flops 8128512 | bytes 33288196 | tf_op jit(solution)/shard_map/reduce_sum | solution.py:58
  251.0 48.7 %all_gather.26 = bf16[8,36,448]{1,0,2:T(8,128)(2,1)S(1)} all-gather(bf16[8,36,7]{1,0,2:T(8,128)(2,1)S(1)} %copy.69), channel_id=1, replica_groups=mesh['buoy'=4,'dom'=64] {'dom'}, dimensions={2}, use_global_device_ids=true | all-gather | bytes 262080 | tf_op jit(solution)/shard_map/all_gather | solution.py:45
  299.7 0.9 copy.70
  300.6 2.8 collective-permute-start.3
  303.4 1.5 collective-permute-start.2
  304.9 5.3 %collective-permute-done.3 = bf16[8,36,448]{2,0,1:T(8,128)(2,1)S(1)} collective-permute-done((bf16[8,36,448]{2,0,1:T(8,128)(2,1)S(1)}, bf16[8,36,448]{2,0,1:T(8,128)(2,1)S(1)}, u32[]{:S(2)}, u32[]{:S(2)}) %collective-permute-start.3) | collective-permute-done | bytes 258080 | tf_op jit(solution)/shard_map/ppermute | solution.py:17
  310.1 4.1 collective-permute-done.2
  314.5 1.0 copy.71
  316.1 0.9 fusion.2
  318.3 0.8 copy-done.2
  319.2 155.6 %all-gather.5.cloned.1.call-done = f32[64,8,36,448]{3,1,2,0:T(8,128)} async-done(((f32[1,8,36,448]{3,1,2,0:T(8,128)}), f32[64,8,36,448]{3,1,2,0:T(8,128)}) %all-gather.5.cloned.1.call-update) | async-done | bytes 33030160 | tf_op jit(solution)/shard_map/all_gather | solution.py:58
  474.8 13.7 %reduce_sum.19 = bf16[8,36,448]{2,0,1:T(8,128)(2,1)S(1)} reduce(f32[64,8,36,448]{3,1,2,0:T(8,128)} %all-gather.5.cloned.1.call-done, f32[]{:T(128)} %constant.34.clone.1), dimensions={0}, to_apply=%region_1.3 | reduce | flops 8128512 | bytes 33288196 | tf_op jit(solution)/shard_map/reduce_sum | solution.py:58
  (46 shorter events, 6.5 us)
Async XLA Ops:
  7.2 71.8 %copy-start = (bf16[2,448,448]{2,1,0:T(8,128)(2,1)S(1)}, bf16[2,448,448]{2,1,0:T(8,128)(2,1)}, u32[]{:S(2)}) copy-start(bf16[2,448,448]{2,1,0:T(8,128)(2,1)} %param.12) | copy-start | bytes 2408452
  7.2 59.6 %copy-start.9 = (s32[2]{0:T(128)S(1)}, s32[2]{0:T(128)}, u32[]{:S(2)}) copy-start(s32[2]{0:T(128)} %param.14) | copy-start | bytes 28
  7.2 59.6 %copy-start.7 = (s32[2]{0:T(128)S(1)}, s32[2]{0:T(128)}, u32[]{:S(2)}) copy-start(s32[2]{0:T(128)} %param.13) | copy-start | bytes 28
  7.2 59.6 %copy-start.6 = (f32[8,36,7]{1,0,2:T(8,128)S(1)}, f32[8,36,7]{1,0,2:T(8,128)}, u32[]{:S(2)}) copy-start(f32[8,36,7]{1,0,2:T(8,128)} %param.10) | copy-start | bytes 24196
  7.2 59.8 %copy-start.10 = (s32[2]{0:T(128)S(1)}, s32[2]{0:T(128)}, u32[]{:S(2)}) copy-start(s32[2]{0:T(128)} %param.15) | copy-start | bytes 28
  7.2 229.9 %all-gather.3.cloned.1.call-start = ((), (), s32[]{:S(2)}) async-start(), calls=%async_computation | async-start | bytes 38338560 | tf_op jit(solution)/shard_map/all_gather | solution.py:58
  62.7 10.2 %collective-permute-start.1 = (bf16[8,36,448]{2,1,0:T(8,128)(2,1)S(1)}, bf16[8,36,448]{2,1,0:T(8,128)(2,1)S(1)}, u32[]{:S(2)}, u32[]{:S(2)}) collective-permute-start(bf16[8,36,448]{2,1,0:T(8,128)(2,1)S(1)} %copy.65), channel_id=1, source_target_pairs={{64,0},{128,64},{192,128},{65,1},{129,65},{193,129},{66,2},{130,66... | collective-permute-start | bytes 774152 | tf_op jit(solution)/shard_map/ppermute | solution.py:17
  65.4 11.7 %collective-permute-start = (bf16[8,36,448]{2,1,0:T(8,128)(2,1)S(1)}, bf16[8,36,448]{2,1,0:T(8,128)(2,1)}, u32[]{:S(2)}, u32[]{:S(2)}) collective-permute-start(bf16[8,36,448]{2,1,0:T(8,128)(2,1)S(1)} %copy.65), channel_id=1, source_target_pairs={{0,64},{64,128},{128,192},{1,65},{65,129},{129,193},{2,66},{66,130... | collective-permute-start | bytes 774152 | tf_op jit(solution)/shard_map/ppermute | solution.py:14
  72.9 0.7 copy-start.4
  81.2 0.8 copy-start.3
  82.0 168.7 %copy-start.8 = (bf16[7,448]{1,0:T(8,128)(2,1)S(1)}, bf16[7,448]{1,0:T(8,128)(2,1)}, u32[]{:S(2)}) copy-start(bf16[7,448]{1,0:T(8,128)(2,1)} %param.16) | copy-start | bytes 18820
  82.0 392.8 %all-gather.5.cloned.1.call-start = ((), (), s32[]{:S(2)}) async-start(), calls=%async_computation.1 | async-start | bytes 38338560 | tf_op jit(solution)/shard_map/all_gather | solution.py:58
  300.6 9.5 %collective-permute-start.3 = (bf16[8,36,448]{2,0,1:T(8,128)(2,1)S(1)}, bf16[8,36,448]{2,0,1:T(8,128)(2,1)S(1)}, u32[]{:S(2)}, u32[]{:S(2)}) collective-permute-start(bf16[8,36,448]{2,0,1:T(8,128)(2,1)S(1)} %copy.70), channel_id=1, source_target_pairs={{64,0},{128,64},{192,128},{65,1},{129,65},{193,129},{66,2},{130,66... | collective-permute-start | bytes 774152 | tf_op jit(solution)/shard_map/ppermute | solution.py:17
  303.4 10.9 %collective-permute-start.2 = (bf16[8,36,448]{2,0,1:T(8,128)(2,1)S(1)}, bf16[8,36,448]{2,0,1:T(8,128)(2,1)S(1)}, u32[]{:S(2)}, u32[]{:S(2)}) collective-permute-start(bf16[8,36,448]{2,0,1:T(8,128)(2,1)S(1)} %copy.70), channel_id=1, source_target_pairs={{0,64},{64,128},{128,192},{1,65},{65,129},{129,193},{2,66},{66,130... | collective-permute-start | bytes 774152 | tf_op jit(solution)/shard_map/ppermute | solution.py:14
  318.3 0.8 copy-start.2
  319.2 170.4 %copy-start.5 = (bf16[128,448]{0,1:T(8,128)(2,1)S(1)}, bf16[128,448]{0,1:T(8,128)(2,1)}, u32[]{:S(2)}) copy-start(bf16[128,448]{0,1:T(8,128)(2,1)} %param.17) | copy-start | bytes 344068
  474.8 15.7 %copy-start.1 = (bf16[2,448,448]{2,1,0:T(8,128)(2,1)S(1)}, bf16[2,448,448]{2,1,0:T(8,128)(2,1)}, u32[]{:S(2)}) copy-start(bf16[2,448,448]{2,1,0:T(8,128)(2,1)} %param.12) | copy-start | bytes 2408452
Sparse Core Ops, SparseCore 0:
  82.2 154.9 all-gather.2
  319.3 155.4 all-gather.4
